TPU v7x, 512 devices: a whole 4x8x8 slice. The times are simulated.
512 devices in a mesh: dp: 16 (over y_lo, x), tile: 32 (over y_hi, z, core).
Axes of the slice: x: 4, y: 8 (y_hi: 2, y_lo: 4; y = y_hi * 4 + y_lo), z: 8, core: 2. Of those that a mesh axis runs over, the one named last changes fastest.
Arguments:
- features: bfloat16 [16, 32, 8, 16, 1024], P('dp', 'tile'), may hold values from -6 to 6
- cotangent: bfloat16 [16, 32, 8, 16, 1024], P('dp', 'tile'), may hold values from -6 to 6
- in_weight: bfloat16 [3072, 1024], P(('dp', 'tile')), may hold values from -0.1875 to 0.1875
- out_weight: bfloat16 [3072, 1024], P(('dp', 'tile')), may hold values from -0.109375 to 0.109375
- hidden_bias: bfloat16 [3072], P(('dp', 'tile')), may hold values from -3 to 3
- kernel: float32 [49, 1024], P(None, 'dp'), may hold values from -0.875 to 0.875
- conv_bias: float32 [1024], P('dp'), may hold values from -3 to 3
- norm_gain: float32 [1024], P('dp'), may hold values from 0.5 to 1.5
- norm_bias: float32 [1024], P('dp'), may hold values from -3 to 3
- layer_scale: float32 [1024], P('dp'), may hold values from 0.5 to 1.5
- out_bias: float32 [1024], P('dp'), may hold values from -3 to 3
Outputs:
- block_out: bfloat16 [16, 32, 8, 16, 1024], P('dp', 'tile')
- grad_input: bfloat16 [16, 32, 8, 16, 1024], P('dp', 'tile')
- grad_kernel: float32 [49, 1024], P(None, 'dp')
- grad_conv_bias: float32 [1024], P('dp')
- grad_norm_gain: float32 [1024], P('dp')
- grad_norm_bias: float32 [1024], P('dp')
- grad_layer_scale: float32 [1024], P('dp')
All inputs are finite; a program needn't handle non-finite values.
Results may differ from a plain program's by a relative error of at most 0.0061.
Values may be sent and summed in bfloat16 or wider, within the bound.
A program may use at most 128 MiB of HBM per device.

v0:
```python
import math
import jax
import jax.numpy as jnp
from jax import lax
from jax.sharding import PartitionSpec as P

KS = 7
GX = 4


def passed_along(block, axis, distance):
    devices = range(lax.axis_size(axis))
    route = [(i - distance, i) for i in devices if i - distance in devices]
    return lax.ppermute(block, axis, route)


def gelu_exact(values):
    return 0.5 * values * (1.0 + jax.scipy.special.erf(values * 0.7071067811865476))


def gelu_slope(values):
    return (
        0.5 * (1.0 + jax.scipy.special.erf(values * 0.7071067811865476))
        + values * jnp.exp(-0.5 * values * values) * 0.3989422804014327
    )


def edge_part(field, step, axis):
    length = field.shape[axis]
    margin = KS // 2
    if step < 0:
        return lax.slice_in_dim(field, length - margin, length, axis=axis)
    if step > 0:
        return lax.slice_in_dim(field, 0, margin, axis=axis)
    return field


def pad_field(field, row_place, col_place, grid_rows):
    bands = []
    for row_step in (-1, 0, 1):
        pieces = []
        for col_step in (-1, 0, 1):
            if row_step == 0 and col_step == 0:
                pieces.append(field)
            else:
                border = edge_part(edge_part(field, row_step, 1), col_step, 2)
                moved = passed_along(border, "tile", -(row_step * GX + col_step))
                row_new = row_place + row_step
                col_new = col_place + col_step
                pieces.append(
                    jnp.where(
                        (row_new >= 0) & (row_new < grid_rows) & (col_new >= 0) & (col_new < GX),
                        moved,
                        jnp.zeros_like(moved),
                    )
                )
        bands.append(jnp.concatenate(pieces, axis=2))
    return jnp.concatenate(bands, axis=1)


def per_device(
    features,
    cotangent,
    in_weight,
    out_weight,
    hidden_bias,
    kernel,
    conv_bias,
    norm_gain,
    norm_bias,
    layer_scale,
    out_bias,
):
    image_count, _, rows, cols, width = features.shape
    tile_count = lax.axis_size("tile")
    grid_rows = tile_count // GX
    place = lax.axis_index("tile")
    row_place = place // GX
    col_place = place % GX
    margin = KS // 2
    kernel_all, cbias, gain, nbias, lscale, obias = (
        lax.all_gather(kernel, "dp", axis=1, tiled=True),
        lax.all_gather(conv_bias, "dp", axis=0, tiled=True),
        lax.all_gather(norm_gain, "dp", axis=0, tiled=True),
        lax.all_gather(norm_bias, "dp", axis=0, tiled=True),
        lax.all_gather(layer_scale, "dp", axis=0, tiled=True),
        lax.all_gather(out_bias, "dp", axis=0, tiled=True),
    )
    picture = features.reshape(image_count, rows, cols, width)
    padded = pad_field(picture, row_place, col_place, grid_rows)
    convolved = jnp.zeros((image_count, rows, cols, width), jnp.float32) + cbias
    for tap_row in range(KS):
        for tap_col in range(KS):
            window = padded[:, tap_row : tap_row + rows, tap_col : tap_col + cols, :].astype(
                jnp.float32
            )
            convolved = convolved + kernel_all[tap_row * KS + tap_col] * window
    average = jnp.mean(convolved, axis=-1, keepdims=True)
    centered = convolved - average
    variance = jnp.mean(centered * centered, axis=-1, keepdims=True)
    inverse = lax.rsqrt(variance + 1e-06)
    pixel_rows = image_count * rows * cols
    standard = (centered * inverse).reshape(pixel_rows, width)
    inverse = inverse.reshape(pixel_rows, 1)
    normed = (standard * gain + nbias).astype(jnp.bfloat16)
    upstream = cotangent.reshape(pixel_rows, width).astype(jnp.float32)
    back_out = (upstream * lscale).astype(jnp.bfloat16)
    rows_in = lax.all_gather(in_weight, ("dp", "tile"), axis=0, tiled=True)
    rows_out = lax.all_gather(out_weight, ("dp", "tile"), axis=0, tiled=True)
    bias_part = lax.all_gather(hidden_bias, ("dp", "tile"), axis=0, tiled=True)
    pre = lax.dot_general(
        normed, rows_in, (((1,), (1,)), ((), ())), preferred_element_type=jnp.float32
    ) + bias_part.astype(jnp.float32)
    hidden = gelu_exact(pre).astype(jnp.bfloat16)
    mlp_sum = jnp.dot(hidden, rows_out, preferred_element_type=jnp.float32)
    back_hidden = lax.dot_general(
        back_out, rows_out, (((1,), (1,)), ((), ())), preferred_element_type=jnp.float32
    )
    back_pre = (back_hidden * gelu_slope(pre)).astype(jnp.bfloat16)
    normed_sum = jnp.dot(back_pre, rows_in, preferred_element_type=jnp.float32)
    mlp_sum, back_normed = (mlp_sum, normed_sum)
    projected = mlp_sum + obias
    source = picture.reshape(pixel_rows, width).astype(jnp.float32)
    block_out = (source + lscale * projected).astype(jnp.bfloat16).reshape(features.shape)
    scale_part = jnp.sum(upstream * projected, axis=0)
    gain_part = jnp.sum(back_normed * standard, axis=0)
    nbias_part = jnp.sum(back_normed, axis=0)
    scaled = back_normed * gain
    back_conv = inverse * (
        scaled
        - jnp.mean(scaled, axis=-1, keepdims=True)
        - standard * jnp.mean(scaled * standard, axis=-1, keepdims=True)
    )
    cbias_part = jnp.sum(back_conv, axis=0)
    back_grid = back_conv.reshape(image_count, rows, cols, width)
    back_padded = pad_field(back_grid.astype(jnp.bfloat16), row_place, col_place, grid_rows)
    grad_grid = upstream.reshape(image_count, rows, cols, width)
    kernel_rows = []
    for tap_row in range(KS):
        for tap_col in range(KS):
            tap_weight = kernel_all[tap_row * KS + tap_col]
            flipped = back_padded[
                :,
                2 * margin - tap_row : 2 * margin - tap_row + rows,
                2 * margin - tap_col : 2 * margin - tap_col + cols,
                :,
            ].astype(jnp.float32)
            grad_grid = grad_grid + tap_weight * flipped
            window = padded[:, tap_row : tap_row + rows, tap_col : tap_col + cols, :].astype(
                jnp.float32
            )
            kernel_rows.append(jnp.sum(back_grid * window, axis=(0, 1, 2)))
    grad_input = grad_grid.astype(jnp.bfloat16).reshape(features.shape)
    kernel_terms = jnp.stack(kernel_rows)
    shared = (
        lax.psum_scatter(kernel_terms, "dp", scatter_dimension=1, tiled=True),
        lax.psum_scatter(cbias_part, "dp", scatter_dimension=0, tiled=True),
        lax.psum_scatter(gain_part, "dp", scatter_dimension=0, tiled=True),
        lax.psum_scatter(nbias_part, "dp", scatter_dimension=0, tiled=True),
        lax.psum_scatter(scale_part, "dp", scatter_dimension=0, tiled=True),
    )
    kernel_sum, cbias_sum, gain_sum, nbias_sum, scale_sum = lax.psum(
        (shared[0], shared[1], shared[2], shared[3], shared[4]), "tile"
    )
    factor = 1.0 / math.sqrt(image_count * lax.axis_size("dp") * rows * cols * tile_count)
    return (
        block_out,
        grad_input,
        kernel_sum * factor,
        cbias_sum * factor,
        gain_sum * factor,
        nbias_sum * factor,
        scale_sum * factor,
    )


def solution(mesh):
    placed = (
        P("dp", "tile", None, None, None),
        P("dp", "tile", None, None, None),
        P(("dp", "tile"), None),
        P(("dp", "tile"), None),
        P(("dp", "tile")),
        P(None, "dp"),
        P("dp"),
        P("dp"),
        P("dp"),
        P("dp"),
        P("dp"),
    )
    return jax.shard_map(
        per_device,
        mesh=mesh,
        in_specs=placed,
        out_specs=(
            P("dp", "tile", None, None, None),
            P("dp", "tile", None, None, None),
            P(None, "dp"),
            P("dp"),
            P("dp"),
            P("dp"),
            P("dp"),
        ),
        check_vma=False,
    )
```

profile of v0, /device:TPU:62, one launch (start us, length us, event | category | flops | bytes accessed | tf_op | source)
XLA Modules:
  0.0 2041.7 jit_solution(7205430439878918634)
XLA Ops:
  9.6 5.5 collective-permute-start
  15.2 9.0 collective-permute-start.7
  24.2 4.6 collective-permute-start.5
  28.8 2.1 collective-permute-start.2
  31.9 3.5 collective-permute-start.3
  35.4 39.3 %all-gather = f32[16,64,49]{1,2,0:T(8,128)S(1)} all-gather(f32[1,64,49]{1,2,0:T(8,128)} %bitcast.363), channel_id=1, replica_groups=mesh['dp'=16,'tile'=32] {'dp'}, dimensions={0}, use_global_device_ids=true | all-gather | bytes 213248 | tf_op jit(solution)/shard_map/all_gather | solution.py:82
  76.5 99.9 %all-reduce.4 = bf16[3072]{0:T(1024)(128)(2,1)S(1)} all-reduce(bf16[3072]{0:T(1024)(128)(2,1)S(1)} %dynamic-update-slice.4), channel_id=1, replica_groups=mesh['dp'=16,'tile'=32] {'dp','tile'}, use_global_device_ids=true, to_apply=%add.4 | all-reduce | flops 3072 | bytes 12288
  179.5 73.9 %all-reduce.12 = (f32[1024]{0:T(1024)S(1)}, f32[1024]{0:T(1024)S(1)}, f32[1024]{0:T(1024)}, f32[1024]{0:T(1024)}, f32[1024]{0:T(1024)}) all-reduce(f32[1024]{0:T(1024)S(1)} %dynamic-update-slice.1, f32[1024]{0:T(1024)S(1)} %dynamic-update-slice.3, f32[1024]{0:T(1024)S(1)} %dynamic-update-slice.2, ...), channel_id=1, replica_groups=mesh['dp'=16,'tile'=32] {'dp'}, use_global_device_ids=true, to_apply=%add.1 | all-reduce | flops 5120 | bytes 40960
  255.3 2.1 collective-permute-start.1
  257.5 10.6 collective-permute-start.6
  268.3 3.1 collective-permute-done.1
  272.1 6.5 fusion.155
  281.1 552.5 %all-gather.6.cloned.1.call-done = bf16[512,6,1024]{2,1,0:T(8,128)(2,1)} async-done(((bf16[1,6,1024]{2,1,0:T(8,128)(2,1)}), bf16[512,6,1024]{2,1,0:T(8,128)(2,1)}) %all-gather.6.cloned.1.call-update) | async-done | bytes 6291472 | tf_op jit(solution)/shard_map/all_gather | solution.py:108
  833.6 11.0 reshape.319
  844.6 5.1 convolution_add_fusion
  849.8 803.6 %all-gather.8.cloned.1.call-done = bf16[512,6,1024]{2,1,0:T(8,128)(2,1)} async-done(((bf16[1,6,1024]{2,1,0:T(8,128)(2,1)}), bf16[512,6,1024]{2,1,0:T(8,128)(2,1)}) %all-gather.8.cloned.1.call-update) | async-done | bytes 6291472 | tf_op jit(solution)/shard_map/all_gather | solution.py:109
  1653.4 11.1 reshape.321
  1664.5 5.3 fusion.133
  1669.7 9.4 fusion.139
  1679.1 2.4 fusion.103
  1683.9 3.7 collective-permute-start.10
  1687.7 73.8 %all-reduce.11 = (f32[1024]{0:T(1024)S(1)}, f32[1024]{0:T(1024)S(1)}, f32[1024]{0:T(1024)S(1)}, f32[1024]{0:T(1024)S(1)}) all-reduce(f32[1024]{0:T(1024)S(1)} %get-tuple-element.62, f32[1024]{0:T(1024)S(1)} %copy-done.83, f32[1024]{0:T(1024)S(1)} %copy-done.84, f32[1024]{0:T(1024)S(1)} %copy-done.80), channel_id=3, replica_groups=mesh['dp'=16,'tile'=32] {'dp'}, use_global_device_ids=true, to_apply=%region_56.57.clone | all-reduce | flops 4096 | bytes 32768
  1763.8 6.5 collective-permute-start.15
  1770.3 6.9 collective-permute-start.12
  1777.2 2.0 collective-permute-start.8
  1781.0 9.6 collective-permute-start.9
  1790.6 1.9 collective-permute-start.11
  1792.6 4.8 collective-permute-start.14
  1798.0 8.3 collective-permute-done.14
  1807.0 5.7 fusion.148
  1812.8 51.9 %reduce-scatter.4.cloned.1.call-done = f32[64,49]{1,0:T(8,128)} async-done(((f32[1024,49]{1,0:T(8,128)}), f32[64,49]{1,0:T(8,128)}) %reduce-scatter.4.cloned.1.call-update) | async-done | bytes 12560
  1865.5 167.0 %all-reduce.10 = (f32[49,64]{1,0:T(8,128)S(1)}, f32[64]{0:T(128)S(1)}, f32[64]{0:T(128)S(1)}, f32[64]{0:T(128)S(1)}, f32[64]{0:T(128)S(1)}) all-reduce(f32[49,64]{1,0:T(8,128)S(1)} %copy.21, f32[64]{0:T(128)S(1)} %dynamic-slice.6, f32[64]{0:T(128)S(1)} %dynamic-slice.8, ...), channel_id=1, replica_groups=mesh['dp'=16,'tile'=32] {'tile'}, use_global_device_ids=true, to_apply=%region_54.55 | all-reduce | flops 3392 | bytes 27136 | tf_op jit(solution)/shard_map/psum | solution.py:162
  (272 shorter events, 22.1 us)
Async XLA Ops:
  7.2 826.4 %all-gather.6.cloned.1.call-start = ((), (), s32[]{:S(2)}) async-start(), calls=%async_computation.1 | async-start | bytes 8404992 | tf_op jit(solution)/shard_map/all_gather | solution.py:108
  7.9 1645.5 %all-gather.8.cloned.1.call-start = ((), (), s32[]{:S(2)}) async-start(), calls=%async_computation.2 | async-start | bytes 8404992 | tf_op jit(solution)/shard_map/all_gather | solution.py:109
  8.7 1856.0 %reduce-scatter.4.cloned.1.call-start = ((), (), s32[]{:S(2)}) async-start(), calls=%async_computation.3 | async-start | bytes 557056
  9.6 243.7 %collective-permute-start = (bf16[1,3,3,1024]{3,2,1,0:T(4,128)(2,1)S(1)}, bf16[1,3,3,1024]{3,2,1,0:T(4,128)(2,1)S(1)}, u32[]{:S(2)}, u32[]{:S(2)}) collective-permute-start(bf16[1,3,3,1024]{3,2,1,0:T(4,128)(2,1)S(1)} %get-tuple-element.105), channel_id=1, source_target_pairs={{0,5},{1,6},{2,7},{3,8},{4,9},{5,10},{6,11},{7,12},{8,13},{9,14},{... | collective-permute-start | bytes 55304 | tf_op jit(solution)/shard_map/ppermute | solution.py:14
  15.2 240.1 %collective-permute-start.7 = (bf16[1,3,3,1024]{3,2,1,0:T(4,128)(2,1)S(1)}, bf16[1,3,3,1024]{3,2,1,0:T(4,128)(2,1)S(1)}, u32[]{:S(2)}, u32[]{:S(2)}) collective-permute-start(bf16[1,3,3,1024]{3,2,1,0:T(4,128)(2,1)S(1)} %get-tuple-element.106), channel_id=1, source_target_pairs={{5,0},{6,1},{7,2},{8,3},{9,4},{10,5},{11,6},{12,7},{13,8},{14,9},{... | collective-permute-start | bytes 55304 | tf_op jit(solution)/shard_map/ppermute | solution.py:14
  24.2 233.3 %collective-permute-start.5 = (bf16[1,3,3,1024]{3,2,1,0:T(4,128)(2,1)S(1)}, bf16[1,3,3,1024]{3,2,1,0:T(4,128)(2,1)S(1)}, u32[]{:S(2)}, u32[]{:S(2)}) collective-permute-start(bf16[1,3,3,1024]{3,2,1,0:T(4,128)(2,1)S(1)} %get-tuple-element.107), channel_id=1, source_target_pairs={{3,0},{4,1},{5,2},{6,3},{7,4},{8,5},{9,6},{10,7},{11,8},{12,9},{13... | collective-permute-start | bytes 55304 | tf_op jit(solution)/shard_map/ppermute | solution.py:14
  28.8 239.3 %collective-permute-start.2 = (bf16[1,3,3,1024]{3,2,1,0:T(4,128)(2,1)S(1)}, bf16[1,3,3,1024]{3,2,1,0:T(4,128)(2,1)S(1)}, u32[]{:S(2)}, u32[]{:S(2)}) collective-permute-start(bf16[1,3,3,1024]{3,2,1,0:T(4,128)(2,1)S(1)} %get-tuple-element.108), channel_id=1, source_target_pairs={{0,3},{1,4},{2,5},{3,6},{4,7},{5,8},{6,9},{7,10},{8,11},{9,12},{10... | collective-permute-start | bytes 55304 | tf_op jit(solution)/shard_map/ppermute | solution.py:14
  31.9 236.3 %collective-permute-start.3 = (bf16[1,8,3,1024]{3,2,1,0:T(4,128)(2,1)S(1)}, bf16[1,8,3,1024]{3,2,1,0:T(4,128)(2,1)S(1)}, u32[]{:S(2)}, u32[]{:S(2)}) collective-permute-start(bf16[1,8,3,1024]{3,2,1,0:T(4,128)(2,1)S(1)} %get-tuple-element.111), channel_id=1, source_target_pairs={{0,1},{1,2},{2,3},{3,4},{4,5},{5,6},{6,7},{7,8},{8,9},{9,10},{10,1... | collective-permute-start | bytes 147464 | tf_op jit(solution)/shard_map/ppermute | solution.py:14
  75.0 196.8 %copy-start.4 = (f32[1,1024]{1,0:T(1,128)}, f32[1,1024]{1,0:T(1,128)S(1)}, u32[]{:S(2)}) copy-start(f32[1,1024]{1,0:T(1,128)S(1)} %get-tuple-element.141) | copy-start | bytes 12292
  75.0 196.8 %copy-start.6 = (f32[1,1024]{1,0:T(1,128)}, f32[1,1024]{1,0:T(1,128)S(1)}, u32[]{:S(2)}) copy-start(f32[1,1024]{1,0:T(1,128)S(1)} %get-tuple-element.142) | copy-start | bytes 12292
  76.1 202.6 %copy-start.62 = (f32[1,1024]{1,0:T(1,128)}, f32[1,1024]{1,0:T(1,128)S(1)}, u32[]{:S(2)}) copy-start(f32[1,1024]{1,0:T(1,128)S(1)} %get-tuple-element.151) | copy-start | bytes 12292
  76.1 202.6 %copy-start.64 = (f32[1,1024]{1,0:T(1,128)}, f32[1,1024]{1,0:T(1,128)S(1)}, u32[]{:S(2)}) copy-start(f32[1,1024]{1,0:T(1,128)S(1)} %get-tuple-element.152) | copy-start | bytes 12292
  76.1 202.6 %copy-start.66 = (f32[1,1024]{1,0:T(1,128)}, f32[1,1024]{1,0:T(1,128)S(1)}, u32[]{:S(2)}) copy-start(f32[1,1024]{1,0:T(1,128)S(1)} %get-tuple-element.153) | copy-start | bytes 12292
  76.1 202.6 %copy-start.68 = (f32[1,1024]{1,0:T(1,128)}, f32[1,1024]{1,0:T(1,128)S(1)}, u32[]{:S(2)}) copy-start(f32[1,1024]{1,0:T(1,128)S(1)} %get-tuple-element.154) | copy-start | bytes 12292
  76.1 202.6 %copy-start.70 = (f32[1,1024]{1,0:T(1,128)}, f32[1,1024]{1,0:T(1,128)S(1)}, u32[]{:S(2)}) copy-start(f32[1,1024]{1,0:T(1,128)S(1)} %get-tuple-element.155) | copy-start | bytes 12292
  76.1 202.6 %copy-start.72 = (f32[1,1024]{1,0:T(1,128)}, f32[1,1024]{1,0:T(1,128)S(1)}, u32[]{:S(2)}) copy-start(f32[1,1024]{1,0:T(1,128)S(1)} %get-tuple-element.156) | copy-start | bytes 12292
  76.1 202.6 %copy-start.74 = (f32[1,1024]{1,0:T(1,128)}, f32[1,1024]{1,0:T(1,128)S(1)}, u32[]{:S(2)}) copy-start(f32[1,1024]{1,0:T(1,128)S(1)} %get-tuple-element.157) | copy-start | bytes 12292
  76.1 202.6 %copy-start.76 = (f32[1,1024]{1,0:T(1,128)}, f32[1,1024]{1,0:T(1,128)S(1)}, u32[]{:S(2)}) copy-start(f32[1,1024]{1,0:T(1,128)S(1)} %get-tuple-element.158) | copy-start | bytes 12292
  76.1 202.6 %copy-start.78 = (f32[1,1024]{1,0:T(1,128)}, f32[1,1024]{1,0:T(1,128)S(1)}, u32[]{:S(2)}) copy-start(f32[1,1024]{1,0:T(1,128)S(1)} %get-tuple-element.159) | copy-start | bytes 12292
  253.4 14.9 collective-permute-start.4
  255.3 16.1 collective-permute-start.1
  257.5 14.0 collective-permute-start.6
  849.7 814.7 %copy-start.81 = (f32[1024]{0:T(1024)S(1)}, f32[1024]{0:T(1024)}, u32[]{:S(2)}) copy-start(f32[1024]{0:T(1024)} %get-tuple-element.85) | copy-start | bytes 12292
  849.8 814.7 %copy-start.82 = (f32[1024]{0:T(1024)S(1)}, f32[1024]{0:T(1024)}, u32[]{:S(2)}) copy-start(f32[1024]{0:T(1024)} %get-tuple-element.86) | copy-start | bytes 12292
  1683.9 97.1 %collective-permute-start.10 = (bf16[1,3,3,1024]{3,2,1,0:T(4,128)(2,1)S(1)}, bf16[1,3,3,1024]{3,2,1,0:T(4,128)(2,1)S(1)}, u32[]{:S(2)}, u32[]{:S(2)}) collective-permute-start(bf16[1,3,3,1024]{3,2,1,0:T(4,128)(2,1)S(1)} %get-tuple-element.97), channel_id=1, source_target_pairs={{3,0},{4,1},{5,2},{6,3},{7,4},{8,5},{9,6},{10,7},{11,8},{12,9},{13... | collective-permute-start | bytes 55304 | tf_op jit(solution)/shard_map/ppermute | solution.py:14
  1761.9 28.7 %collective-permute-start.13 = (bf16[1,3,3,1024]{3,2,1,0:T(4,128)(2,1)S(1)}, bf16[1,3,3,1024]{3,2,1,0:T(4,128)(2,1)S(1)}, u32[]{:S(2)}, u32[]{:S(2)}) collective-permute-start(bf16[1,3,3,1024]{3,2,1,0:T(4,128)(2,1)S(1)} %get-tuple-element.98), channel_id=1, source_target_pairs={{0,5},{1,6},{2,7},{3,8},{4,9},{5,10},{6,11},{7,12},{8,13},{9,14},{... | collective-permute-start | bytes 55304 | tf_op jit(solution)/shard_map/ppermute | solution.py:14
  1763.8 28.8 %collective-permute-start.15 = (bf16[1,3,3,1024]{3,2,1,0:T(4,128)(2,1)S(1)}, bf16[1,3,3,1024]{3,2,1,0:T(4,128)(2,1)S(1)}, u32[]{:S(2)}, u32[]{:S(2)}) collective-permute-start(bf16[1,3,3,1024]{3,2,1,0:T(4,128)(2,1)S(1)} %get-tuple-element.99), channel_id=1, source_target_pairs={{0,3},{1,4},{2,5},{3,6},{4,7},{5,8},{6,9},{7,10},{8,11},{9,12},{10... | collective-permute-start | bytes 55304 | tf_op jit(solution)/shard_map/ppermute | solution.py:14
  1770.3 27.2 %collective-permute-start.12 = (bf16[1,3,3,1024]{3,2,1,0:T(4,128)(2,1)S(1)}, bf16[1,3,3,1024]{3,2,1,0:T(4,128)(2,1)S(1)}, u32[]{:S(2)}, u32[]{:S(2)}) collective-permute-start(bf16[1,3,3,1024]{3,2,1,0:T(4,128)(2,1)S(1)} %get-tuple-element.100), channel_id=1, source_target_pairs={{5,0},{6,1},{7,2},{8,3},{9,4},{10,5},{11,6},{12,7},{13,8},{14,9},{... | collective-permute-start | bytes 55304 | tf_op jit(solution)/shard_map/ppermute | solution.py:14
  1777.2 20.3 collective-permute-start.8
  1781.0 16.5 collective-permute-start.9
  1790.6 7.4 collective-permute-start.11
  1792.6 13.7 collective-permute-start.14
  (79 other events, 7366.8 us)
Sparse Core Ops, SparseCore 0:
  10.2 823.3 all-gather.5
  835.8 817.5 all-gather.7
  1781.1 83.4 reduce-scatter.3
where the time goes:
time: 2040 us
  waiting for transfers between devices  1420 us (70%)
  blocking collectives  454 us (22%)
  starting transfers between devices  76.7 us (4%)
  local copies, waits for them, and re-layouts  30.7 us (2%)
  other arithmetic  22.4 us (1%)
    all_gather x1, waiting for transfers between devices, per_device(): rows_out = lax.all_gather(out_weight, ('dp', 'tile'), axis=0, tiled=True)  804 us
    all_gather x1, waiting for transfers between devices, per_device(): rows_in = lax.all_gather(in_weight, ('dp', 'tile'), axis=0, tiled=True)  552 us
    unnamed x3, blocking collectives  248 us
    psum x1, blocking collectives, per_device(): lax.psum((shared[0], shared[1], shared[2], shared[3], shared[4]), 'tile')  167 us
    ppermute x16, starting transfers between devices, passed_along(): return lax.ppermute(block, axis, route)  76.6 us
    unnamed x4, waiting for transfers between devices  53.3 us
  transfers between devices with their start and end apart: 19, of which 6 were waited for; matrix products, arithmetic and copies ran while one was open for 2% of the time, Pallas kernels for 0%

commit v1 on v0

--- a/solution.py
+++ b/solution.py
@@ -106,7 +106,9 @@
     upstream = cotangent.reshape(pixel_rows, width).astype(jnp.float32)
     back_out = (upstream * lscale).astype(jnp.bfloat16)
     rows_in = lax.all_gather(in_weight, ("dp", "tile"), axis=0, tiled=True)
-    rows_out = lax.all_gather(out_weight, ("dp", "tile"), axis=0, tiled=True)
+    n_now = jnp.stack([out_weight for _ in range(lax.axis_size(("dp", "tile")))], 0)
+    g_now = lax.all_to_all(n_now, ("dp", "tile"), 0, 0)
+    rows_out = jnp.concatenate(g_now, 0)
     bias_part = lax.all_gather(hidden_bias, ("dp", "tile"), axis=0, tiled=True)
     pre = lax.dot_general(
         normed, rows_in, (((1,), (1,)), ((), ())), preferred_element_type=jnp.float32

time: 2040 us -> 1360 us (0.67)
  the two profiles are of different devices: /device:TPU:62 before, /device:TPU:32 now
where the time goes in v1:
time: 1360 us
  blocking collectives  629 us (46%)
  waiting for transfers between devices  553 us (41%)
  starting transfers between devices  84.8 us (6%)
  local copies, waits for them, and re-layouts  36 us (3%)
  other arithmetic  25 us (2%)
  between operations  17.8 us (1%)
  matrix products  16.5 us (1%)
    all_gather x1, waiting for transfers between devices, per_device(): rows_in = lax.all_gather(in_weight, ('dp', 'tile'), axis=0, tiled=True)  534 us
    unnamed x3, blocking collectives  263 us
    all_gather x1, blocking collectives, per_device(): lax.all_gather(kernel, 'dp', axis=1, tiled=True)  199 us
    psum x1, blocking collectives, per_device(): lax.psum((shared[0], shared[1], shared[2], shared[3], shared[4]), 'tile')  167 us
    ppermute x16, starting transfers between devices, passed_along(): return lax.ppermute(block, axis, route)  61.7 us
  transfers between devices with their start and end apart: 19, of which 4 were waited for; matrix products, arithmetic and copies ran while one was open for 3% of the time, Pallas kernels for 0%

profile of v1, /device:TPU:32, one launch (start us, length us, event | category | flops | bytes accessed | tf_op | source)
XLA Modules:
  0.0 1361.6 jit_solution(13693805816076579156)
XLA Ops:
  7.9 5.0 stack.102
  12.9 23.0 %all-to-all-start = ((bf16[512,6,1024]{2,1,0:T(8,128)(2,1)}), bf16[512,6,1024]{2,1,0:T(8,128)(2,1)}, u32[]{:S(2)}, u32[]{:S(2)}) async-start(bf16[512,6,1024]{2,1,0:T(8,128)(2,1)} %stack.102), calls=%async_computation | async-start | bytes 16777216 | tf_op jit(solution)/shard_map/all_to_all | solution.py:110
  36.1 7.8 collective-permute-start.4
  43.9 1.9 collective-permute-start.3
  45.9 1.9 collective-permute-start.2
  47.9 4.3 collective-permute-start.1
  52.2 3.4 collective-permute-start
  55.6 198.8 %all-gather = f32[16,64,49]{1,2,0:T(8,128)S(1)} all-gather(f32[1,64,49]{1,2,0:T(8,128)S(1)} %bitcast.361), channel_id=1, replica_groups=mesh['dp'=16,'tile'=32] {'dp'}, dimensions={0}, use_global_device_ids=true | all-gather | bytes 213248 | tf_op jit(solution)/shard_map/all_gather | solution.py:82
  257.2 76.4 %all-reduce.12 = (f32[1024]{0:T(1024)S(1)}, f32[1024]{0:T(1024)S(1)}, f32[1024]{0:T(1024)}, f32[1024]{0:T(1024)}, f32[1024]{0:T(1024)S(1)}) all-reduce(f32[1024]{0:T(1024)S(1)} %dynamic-update-slice.1, f32[1024]{0:T(1024)S(1)} %dynamic-update-slice.3, f32[1024]{0:T(1024)S(1)} %dynamic-update-slice.2, ...), channel_id=1, replica_groups=mesh['dp'=16,'tile'=32] {'dp'}, use_global_device_ids=true, to_apply=%add.1 | all-reduce | flops 5120 | bytes 40960
  335.8 101.6 %all-reduce.4 = bf16[3072]{0:T(1024)(128)(2,1)S(1)} all-reduce(bf16[3072]{0:T(1024)(128)(2,1)S(1)} %dynamic-update-slice.4), channel_id=1, replica_groups=mesh['dp'=16,'tile'=32] {'dp','tile'}, use_global_device_ids=true, to_apply=%add.4 | all-reduce | flops 3072 | bytes 12288
  438.0 4.9 collective-permute-start.7
  443.0 3.8 collective-permute-start.6
  446.8 7.8 collective-permute-start.5
  456.8 6.5 fusion.153
  465.8 534.1 %all-gather.4.cloned.1.call-done = bf16[512,6,1024]{2,1,0:T(8,128)(2,1)} async-done(((bf16[1,6,1024]{2,1,0:T(8,128)(2,1)}), bf16[512,6,1024]{2,1,0:T(8,128)(2,1)}) %all-gather.4.cloned.1.call-update) | async-done | bytes 6291472 | tf_op jit(solution)/shard_map/all_gather | solution.py:108
  999.8 11.1 reshape.330
  1010.9 5.1 convolution_add_fusion
  1016.0 11.1 reshape.303
  1027.1 9.3 fusion.137
  1036.4 3.2 fusion.103
  1044.0 2.1 fusion.106
  1046.1 2.0 collective-permute-start.12
  1048.2 7.3 collective-permute-start.11
  1055.5 4.2 collective-permute-start.10
  1059.7 1.9 collective-permute-start.9
  1061.6 2.4 collective-permute-start.8
  1067.5 84.7 %all-reduce.11 = (f32[1024]{0:T(1024)S(1)}, f32[1024]{0:T(1024)S(1)}, f32[1024]{0:T(1024)S(1)}, f32[1024]{0:T(1024)S(1)}) all-reduce(f32[1024]{0:T(1024)S(1)} %get-tuple-element.97, f32[1024]{0:T(1024)} %get-tuple-element.49, f32[1024]{0:T(1024)} %get-tuple-element.61, ...), channel_id=3, replica_groups=mesh['dp'=16,'tile'=32] {'dp'}, use_global_device_ids=true, to_apply=%region_56.57.clone | all-reduce | flops 4096 | bytes 32768
  1154.5 4.2 collective-permute-start.14
  1158.7 5.9 collective-permute-done.15
  1166.5 11.0 collective-permute-done.13
  1178.5 5.8 fusion.146
  1185.1 167.0 %all-reduce.10 = (f32[49,64]{1,0:T(8,128)S(1)}, f32[64]{0:T(128)S(1)}, f32[64]{0:T(128)S(1)}, f32[64]{0:T(128)S(1)}, f32[64]{0:T(128)S(1)}) all-reduce(f32[49,64]{1,0:T(8,128)S(1)} %copy.21, f32[64]{0:T(128)S(1)} %dynamic-slice.6, f32[64]{0:T(128)S(1)} %dynamic-slice.8, ...), channel_id=1, replica_groups=mesh['dp'=16,'tile'=32] {'tile'}, use_global_device_ids=true, to_apply=%region_54.55 | all-reduce | flops 3392 | bytes 27136 | tf_op jit(solution)/shard_map/psum | solution.py:164
  (345 shorter events, 24.4 us)
Async XLA Ops:
  7.2 992.7 %all-gather.4.cloned.1.call-start = ((), (), s32[]{:S(2)}) async-start(), calls=%async_computation.2 | async-start | bytes 8404992 | tf_op jit(solution)/shard_map/all_gather | solution.py:108
  12.9 1003.1 %all-to-all-start = ((bf16[512,6,1024]{2,1,0:T(8,128)(2,1)}), bf16[512,6,1024]{2,1,0:T(8,128)(2,1)}, u32[]{:S(2)}, u32[]{:S(2)}) async-start(bf16[512,6,1024]{2,1,0:T(8,128)(2,1)} %stack.102), calls=%async_computation | async-start | bytes 16777216 | tf_op jit(solution)/shard_map/all_to_all | solution.py:110
  35.9 218.8 %copy-start.119 = (u32[512]{0:T(512)S(1)}, u32[512]{0:T(512)}, u32[]{:S(2)}) copy-start(u32[512]{0:T(512)} %constant.70) | copy-start | bytes 6148
  35.9 220.1 %copy-start.120 = (f32[64]{0:T(128)S(1)}, f32[64]{0:T(128)}, u32[]{:S(2)}) copy-start(f32[64]{0:T(128)} %param.17) | copy-start | bytes 772
  35.9 220.3 %copy-start.121 = (f32[64]{0:T(128)S(1)}, f32[64]{0:T(128)}, u32[]{:S(2)}) copy-start(f32[64]{0:T(128)} %param.19) | copy-start | bytes 772
  35.9 220.6 %copy-start.122 = (f32[64]{0:T(128)S(1)}, f32[64]{0:T(128)}, u32[]{:S(2)}) copy-start(f32[64]{0:T(128)} %param.18) | copy-start | bytes 772
  35.9 220.8 %copy-start.123 = (f32[64]{0:T(128)S(1)}, f32[64]{0:T(128)}, u32[]{:S(2)}) copy-start(f32[64]{0:T(128)} %param.21) | copy-start | bytes 772
  35.9 221.0 %copy-start.124 = (f32[64]{0:T(128)S(1)}, f32[64]{0:T(128)}, u32[]{:S(2)}) copy-start(f32[64]{0:T(128)} %param.20) | copy-start | bytes 772
  36.0 1148.3 %reduce-scatter.4.cloned.1.call-start = ((), (), s32[]{:S(2)}) async-start(), calls=%async_computation.3 | async-start | bytes 557056
  36.0 298.0 %copy-start.1 = (bf16[1,1,8,16,1024]{4,3,2,1,0:T(8,128)(2,1)S(1)}, bf16[1,1,8,16,1024]{4,3,2,1,0:T(8,128)(2,1)}, u32[]{:S(2)}) copy-start(bf16[1,1,8,16,1024]{4,3,2,1,0:T(8,128)(2,1)} %param.12) | copy-start | bytes 786436
  36.1 419.9 %collective-permute-start.4 = (bf16[1,8,3,1024]{3,2,1,0:T(4,128)(2,1)S(1)}, bf16[1,8,3,1024]{3,2,1,0:T(4,128)(2,1)S(1)}, u32[]{:S(2)}, u32[]{:S(2)}) collective-permute-start(bf16[1,8,3,1024]{3,2,1,0:T(4,128)(2,1)S(1)} %get-tuple-element.113), channel_id=1, source_target_pairs={{1,0},{2,1},{3,2},{4,3},{5,4},{6,5},{7,6},{8,7},{9,8},{10,9},{11,1... | collective-permute-start | bytes 147464 | tf_op jit(solution)/shard_map/ppermute | solution.py:14
  43.9 412.1 %collective-permute-start.3 = (bf16[1,8,3,1024]{3,2,1,0:T(4,128)(2,1)S(1)}, bf16[1,8,3,1024]{3,2,1,0:T(4,128)(2,1)S(1)}, u32[]{:S(2)}, u32[]{:S(2)}) collective-permute-start(bf16[1,8,3,1024]{3,2,1,0:T(4,128)(2,1)S(1)} %get-tuple-element.112), channel_id=1, source_target_pairs={{0,1},{1,2},{2,3},{3,4},{4,5},{5,6},{6,7},{7,8},{8,9},{9,10},{10,1... | collective-permute-start | bytes 147464 | tf_op jit(solution)/shard_map/ppermute | solution.py:14
  45.9 392.1 %collective-permute-start.2 = (bf16[1,3,3,1024]{3,2,1,0:T(4,128)(2,1)S(1)}, bf16[1,3,3,1024]{3,2,1,0:T(4,128)(2,1)S(1)}, u32[]{:S(2)}, u32[]{:S(2)}) collective-permute-start(bf16[1,3,3,1024]{3,2,1,0:T(4,128)(2,1)S(1)} %get-tuple-element.109), channel_id=1, source_target_pairs={{0,3},{1,4},{2,5},{3,6},{4,7},{5,8},{6,9},{7,10},{8,11},{9,12},{10... | collective-permute-start | bytes 55304 | tf_op jit(solution)/shard_map/ppermute | solution.py:14
  47.9 287.7 %copy-start.125 = (bf16[6]{0:T(256)(128)(2,1)S(1)}, bf16[6]{0:T(256)(128)(2,1)}, u32[]{:S(2)}) copy-start(bf16[6]{0:T(256)(128)(2,1)} %param.15) | copy-start | bytes 40
  47.9 408.2 %collective-permute-start.1 = (bf16[1,3,16,1024]{3,2,1,0:T(8,128)(2,1)S(1)}, bf16[1,3,16,1024]{3,2,1,0:T(8,128)(2,1)S(1)}, u32[]{:S(2)}, u32[]{:S(2)}) collective-permute-start(bf16[1,3,16,1024]{3,2,1,0:T(8,128)(2,1)S(1)} %get-tuple-element.110), channel_id=1, source_target_pairs={{0,4},{1,5},{2,6},{3,7},{4,8},{5,9},{6,10},{7,11},{8,12},{9,13},{1... | collective-permute-start | bytes 294920 | tf_op jit(solution)/shard_map/ppermute | solution.py:14
  52.2 390.7 %collective-permute-start = (bf16[1,3,3,1024]{3,2,1,0:T(4,128)(2,1)S(1)}, bf16[1,3,3,1024]{3,2,1,0:T(4,128)(2,1)S(1)}, u32[]{:S(2)}, u32[]{:S(2)}) collective-permute-start(bf16[1,3,3,1024]{3,2,1,0:T(4,128)(2,1)S(1)} %get-tuple-element.106), channel_id=1, source_target_pairs={{0,5},{1,6},{2,7},{3,8},{4,9},{5,10},{6,11},{7,12},{8,13},{9,14},{... | collective-permute-start | bytes 55304 | tf_op jit(solution)/shard_map/ppermute | solution.py:14
  335.4 127.9 %copy-start.71 = (f32[1,1024]{1,0:T(1,128)}, f32[1,1024]{1,0:T(1,128)S(1)}, u32[]{:S(2)}) copy-start(f32[1,1024]{1,0:T(1,128)S(1)} %get-tuple-element.156) | copy-start | bytes 12292
  335.4 127.9 %copy-start.73 = (f32[1,1024]{1,0:T(1,128)}, f32[1,1024]{1,0:T(1,128)S(1)}, u32[]{:S(2)}) copy-start(f32[1,1024]{1,0:T(1,128)S(1)} %get-tuple-element.157) | copy-start | bytes 12292
  335.4 127.9 %copy-start.75 = (f32[1,1024]{1,0:T(1,128)}, f32[1,1024]{1,0:T(1,128)S(1)}, u32[]{:S(2)}) copy-start(f32[1,1024]{1,0:T(1,128)S(1)} %get-tuple-element.158) | copy-start | bytes 12292
  335.4 127.9 %copy-start.77 = (f32[1,1024]{1,0:T(1,128)}, f32[1,1024]{1,0:T(1,128)S(1)}, u32[]{:S(2)}) copy-start(f32[1,1024]{1,0:T(1,128)S(1)} %get-tuple-element.159) | copy-start | bytes 12292
  335.4 127.9 %copy-start.79 = (f32[1,1024]{1,0:T(1,128)}, f32[1,1024]{1,0:T(1,128)S(1)}, u32[]{:S(2)}) copy-start(f32[1,1024]{1,0:T(1,128)S(1)} %get-tuple-element.160) | copy-start | bytes 12292
  438.0 8.8 collective-permute-start.7
  443.0 13.2 collective-permute-start.6
  446.8 9.1 collective-permute-start.5
  1046.1 106.4 %collective-permute-start.12 = (bf16[1,3,3,1024]{3,2,1,0:T(4,128)(2,1)}, bf16[1,3,3,1024]{3,2,1,0:T(4,128)(2,1)S(1)}, u32[]{:S(2)}, u32[]{:S(2)}) collective-permute-start(bf16[1,3,3,1024]{3,2,1,0:T(4,128)(2,1)} %get-tuple-element.101), channel_id=1, source_target_pairs={{5,0},{6,1},{7,2},{8,3},{9,4},{10,5},{11,6},{12,7},{13,8},{14,9},{... | collective-permute-start | bytes 55304 | tf_op jit(solution)/shard_map/ppermute | solution.py:14
  1048.2 129.5 %collective-permute-start.11 = (bf16[1,3,16,1024]{3,2,1,0:T(8,128)(2,1)S(1)}, bf16[1,3,16,1024]{3,2,1,0:T(8,128)(2,1)S(1)}, u32[]{:S(2)}, u32[]{:S(2)}) collective-permute-start(bf16[1,3,16,1024]{3,2,1,0:T(8,128)(2,1)S(1)} %get-tuple-element.102), channel_id=1, source_target_pairs={{4,0},{5,1},{6,2},{7,3},{8,4},{9,5},{10,6},{11,7},{12,8},{13,9},{1... | collective-permute-start | bytes 294920 | tf_op jit(solution)/shard_map/ppermute | solution.py:14
  1055.5 98.9 %collective-permute-start.10 = (bf16[1,3,3,1024]{3,2,1,0:T(4,128)(2,1)}, bf16[1,3,3,1024]{3,2,1,0:T(4,128)(2,1)S(1)}, u32[]{:S(2)}, u32[]{:S(2)}) collective-permute-start(bf16[1,3,3,1024]{3,2,1,0:T(4,128)(2,1)} %get-tuple-element.98), channel_id=1, source_target_pairs={{3,0},{4,1},{5,2},{6,3},{7,4},{8,5},{9,6},{10,7},{11,8},{12,9},{13... | collective-permute-start | bytes 55304 | tf_op jit(solution)/shard_map/ppermute | solution.py:14
  1059.7 117.9 %collective-permute-start.9 = (bf16[1,8,3,1024]{3,2,1,0:T(4,128)(2,1)S(1)}, bf16[1,8,3,1024]{3,2,1,0:T(4,128)(2,1)S(1)}, u32[]{:S(2)}, u32[]{:S(2)}) collective-permute-start(bf16[1,8,3,1024]{3,2,1,0:T(4,128)(2,1)S(1)} %get-tuple-element.105), channel_id=1, source_target_pairs={{1,0},{2,1},{3,2},{4,3},{5,4},{6,5},{7,6},{8,7},{9,8},{10,9},{11,1... | collective-permute-start | bytes 147464 | tf_op jit(solution)/shard_map/ppermute | solution.py:14
  1061.6 116.0 %collective-permute-start.8 = (bf16[1,8,3,1024]{3,2,1,0:T(4,128)(2,1)S(1)}, bf16[1,8,3,1024]{3,2,1,0:T(4,128)(2,1)S(1)}, u32[]{:S(2)}, u32[]{:S(2)}) collective-permute-start(bf16[1,8,3,1024]{3,2,1,0:T(4,128)(2,1)S(1)} %get-tuple-element.104), channel_id=1, source_target_pairs={{0,1},{1,2},{2,3},{3,4},{4,5},{5,6},{6,7},{7,8},{8,9},{9,10},{10,1... | collective-permute-start | bytes 147464 | tf_op jit(solution)/shard_map/ppermute | solution.py:14
  1152.5 12.1 collective-permute-start.15
  1154.5 23.3 %collective-permute-start.14 = (bf16[1,3,16,1024]{3,2,1,0:T(8,128)(2,1)S(1)}, bf16[1,3,16,1024]{3,2,1,0:T(8,128)(2,1)S(1)}, u32[]{:S(2)}, u32[]{:S(2)}) collective-permute-start(bf16[1,3,16,1024]{3,2,1,0:T(8,128)(2,1)S(1)} %get-tuple-element.103), channel_id=1, source_target_pairs={{0,4},{1,5},{2,6},{3,7},{4,8},{5,9},{6,10},{7,11},{8,12},{9,13},{1... | collective-permute-start | bytes 294920 | tf_op jit(solution)/shard_map/ppermute | solution.py:14
  1164.6 12.9 collective-permute-start.13
  (115 other events, 9259.5 us)
Sparse Core Ops, SparseCore 0:
  10.2 989.5 all-gather.3
  1067.6 91.1 reduce-scatter.3
